TPU v7x, 512 devices: a whole 4x4x16 slice. The times are simulated.
512 devices in a mesh: dp: 16 (over z), segment: 2 (over y_hi), tensor: 16 (over x, y_lo, core).
Axes of the slice: x: 4, y: 4 (y_hi: 2, y_lo: 2; y = y_hi * 2 + y_lo), z: 16, core: 2. Of those that a mesh axis runs over, the one named last changes fastest.
Arguments:
- context: bfloat16 [1152, 4096], P(None, 'tensor'), may hold values from -6 to 6
- residual: bfloat16 [1152, 4096], P(None, 'dp'), may hold values from -6 to 6
- inverse_rms: float32 [1152], replicated, may hold values from 0.5 to 2
- norm_gain: float32 [4096], P('dp'), may hold values from 0.5 to 1.5
- gate_preact: bfloat16 [1152, 14336], P(None, 'tensor'), may hold values from -6 to 6
- up_preact: bfloat16 [1152, 14336], P(None, 'tensor'), may hold values from -6 to 6
- upstream: bfloat16 [1152, 4096], P(None, 'dp'), may hold values from -6 to 6
- gate_weight: bfloat16 [4096, 14336], P('dp', 'tensor'), may hold values from -0.09375 to 0.09375
- up_weight: bfloat16 [4096, 14336], P('dp', 'tensor'), may hold values from -0.09375 to 0.09375
- down_weight: bfloat16 [14336, 4096], P('tensor', 'dp'), may hold values from -0.046875 to 0.046875
- policy_logprob: float32 [32], replicated, may hold values from -270 to -230
- ref_logprob: float32 [32], replicated, may hold values from -270 to -230
- lengths: int32 [32], replicated, may hold values from 4061 to 4096
Outputs:
- residual_grad: bfloat16 [1152, 4096], P('tensor', 'dp')
- output_weight_grad: bfloat16 [4096, 4096], P('tensor', ('dp', 'segment'))
- gate_weight_grad: bfloat16 [4096, 14336], P(('dp', 'segment'), 'tensor')
- up_weight_grad: bfloat16 [4096, 14336], P(('dp', 'segment'), 'tensor')
- down_weight_grad: bfloat16 [14336, 4096], P('tensor', ('dp', 'segment'))
Inputs may be any that keep to these rules, and one draw needn't show every extreme that they name: `lengths`: the window holds positions 4060 to 4095 of every sequence; a position counts where it is below the sequence's length.
All inputs are finite; a program needn't handle non-finite values.
Results may differ from a plain program's by a relative error of at most 0.03.
Values may be sent and summed in bfloat16 or wider, within the bound.
A program may use at most 64 MiB of HBM per device.

v0:
```python
import jax
import jax.numpy as jnp
from jax import lax
from jax.sharding import PartitionSpec as P

D = 4096
POS = 36
LEN = 4096


def shifted(value, axis, steps):
    count = lax.axis_size(axis)
    first, last = (max(0, -steps), min(count, count - steps))
    return lax.ppermute(value, axis, [(source, source + steps) for source in range(first, last)])


def from_partner(value, axis, apart):
    mask = 2**apart
    pairs = [(source, source ^ mask) for source in range(lax.axis_size(axis))]
    return lax.ppermute(value, axis, pairs)


def token_weights(policy_logprob, ref_logprob, lengths, total_rows):
    npo_weight = 2.0 * jax.nn.sigmoid(0.1 * (policy_logprob - ref_logprob))
    positions = jnp.arange(total_rows, dtype=jnp.int32)
    sequence_of = positions // POS
    position_in = LEN - POS + positions % POS
    member = sequence_of[:, None] == jnp.arange(policy_logprob.shape[0], dtype=jnp.int32)[None, :]
    weight = jnp.sum(jnp.where(member, npo_weight[None, :], 0.0), axis=1)
    length_of = jnp.sum(jnp.where(member, lengths[None, :], 0), axis=1)
    return jnp.where(position_in < length_of, weight, 0.0)


def gate_grads_of(hidden_delta, gate_value, up_value):
    squash = jax.nn.sigmoid(gate_value)
    gate_delta = (hidden_delta * up_value * squash * (1.0 + gate_value * (1.0 - squash))).astype(
        jnp.bfloat16
    )
    up_delta = (hidden_delta * gate_value * squash).astype(jnp.bfloat16)
    return (gate_delta, up_delta)


def row_statistic(partial_dot):
    return lax.psum(partial_dot, "dp")


def finish_rows(weighted, residual, inverse_rms, norm_gain, normed_delta):
    residual_value = residual.astype(jnp.float32)
    row_dot = row_statistic(jnp.sum(norm_gain[None, :] * normed_delta * residual_value, axis=1))
    row_scale = inverse_rms * inverse_rms * inverse_rms * row_dot / D
    combined = (
        weighted.astype(jnp.float32)
        + inverse_rms[:, None] * norm_gain[None, :] * normed_delta
        - residual_value * row_scale[:, None]
    )
    return combined.astype(jnp.bfloat16)


def shards(
    context,
    residual,
    inverse_rms,
    norm_gain,
    gate_preact,
    up_preact,
    upstream,
    gate_weight,
    up_weight,
    down_weight,
    policy_logprob,
    ref_logprob,
    lengths,
):
    ffn_side = lax.axis_index("segment") == 1
    total_rows = residual.shape[0]
    features = residual.shape[1]
    hidden_width = gate_preact.shape[1]
    half_width = features // 2
    share_rows = total_rows // lax.axis_size("tensor")
    share_start = lax.axis_index("tensor") * share_rows
    token_weight = token_weights(policy_logprob, ref_logprob, lengths, total_rows)
    weighted = (upstream.astype(jnp.float32) * token_weight[:, None]).astype(jnp.bfloat16)
    normed = (residual.astype(jnp.float32) * inverse_rms[:, None] * norm_gain[None, :]).astype(
        jnp.bfloat16
    )
    gate_value = gate_preact.astype(jnp.float32)
    up_value = up_preact.astype(jnp.float32)
    hidden = (gate_value * jax.nn.sigmoid(gate_value) * up_value).astype(jnp.bfloat16)

    def down_part():
        return jnp.einsum("tf,td->fd", hidden, weighted, preferred_element_type=jnp.float32)

    down_full = lax.cond(
        ffn_side, down_part, lambda: jnp.zeros((hidden_width, features), jnp.float32)
    )
    hidden_delta = lax.psum(
        lax.cond(
            ffn_side,
            lambda: jnp.einsum(
                "td,fd->tf", weighted, down_weight, preferred_element_type=jnp.float32
            ),
            lambda: jnp.zeros((total_rows, hidden_width), jnp.float32),
        ).astype(jnp.bfloat16),
        "dp",
    ).astype(jnp.float32)
    gate_delta, up_delta = gate_grads_of(hidden_delta, gate_value, up_value)

    def weight_parts():
        gate_full = jnp.einsum("td,tf->df", normed, gate_delta, preferred_element_type=jnp.float32)
        up_full = jnp.einsum("td,tf->df", normed, up_delta, preferred_element_type=jnp.float32)
        return (gate_full, up_full)

    empty_grad = jnp.zeros((features, hidden_width), jnp.float32)
    gate_full, up_full = lax.cond(ffn_side, weight_parts, lambda: (empty_grad, empty_grad))

    def product():
        first_term = jnp.einsum(
            "tf,df->td", gate_delta, gate_weight, preferred_element_type=jnp.float32
        )
        return first_term + jnp.einsum(
            "tf,df->td", up_delta, up_weight, preferred_element_type=jnp.float32
        )

    normed_delta = lax.psum(
        lax.cond(ffn_side, product, lambda: jnp.zeros((total_rows, features), jnp.float32)).astype(
            jnp.bfloat16
        ),
        "tensor",
    ).astype(jnp.float32)
    grad_every = finish_rows(weighted, residual, inverse_rms, norm_gain, normed_delta)
    arrived = shifted(grad_every, "segment", -1)
    grad_tokens = jnp.where(ffn_side, grad_every, arrived)
    residual_grad = lax.dynamic_slice_in_dim(grad_tokens, share_start, share_rows, 0)

    def projection_part():
        return jnp.einsum("tc,td->cd", context, grad_tokens, preferred_element_type=jnp.float32)

    projection_full = lax.cond(
        ffn_side, lambda: jnp.zeros((context.shape[1], features), jnp.float32), projection_part
    )
    projection_bf = projection_full.astype(jnp.bfloat16)
    gate_bf = gate_full.astype(jnp.bfloat16)
    up_bf = up_full.astype(jnp.bfloat16)
    down_bf = down_full.astype(jnp.bfloat16)
    got_projection, got_gate, got_up, got_down = from_partner(
        (
            projection_bf[:, half_width:],
            gate_bf[:half_width],
            up_bf[:half_width],
            down_bf[:, :half_width],
        ),
        "segment",
        0,
    )
    output_weight_grad = jnp.where(ffn_side, got_projection, projection_bf[:, :half_width])
    gate_weight_grad = jnp.where(ffn_side, gate_bf[half_width:], got_gate)
    up_weight_grad = jnp.where(ffn_side, up_bf[half_width:], got_up)
    down_weight_grad = jnp.where(ffn_side, down_bf[:, half_width:], got_down)
    return (residual_grad, output_weight_grad, gate_weight_grad, up_weight_grad, down_weight_grad)


def solution(mesh):
    return jax.shard_map(
        shards,
        mesh=mesh,
        in_specs=(
            P(None, "tensor"),
            P(None, "dp"),
            P(),
            P("dp"),
            P(None, "tensor"),
            P(None, "tensor"),
            P(None, "dp"),
            P("dp", "tensor"),
            P("dp", "tensor"),
            P("tensor", "dp"),
            P(),
            P(),
            P(),
        ),
        out_specs=(
            P("tensor", "dp"),
            P("tensor", ("dp", "segment")),
            P(("dp", "segment"), "tensor"),
            P(("dp", "segment"), "tensor"),
            P("tensor", ("dp", "segment")),
        ),
        check_vma=False,
    )
```

profile of v0, /device:TPU:14, one launch (start us, length us, event | category | flops | bytes accessed | tf_op | source)
XLA Modules:
  0.0 375.4 jit_solution(5367766257168562192)
XLA Ops:
  7.2 0.7 divide_multiply_fusion
  7.9 0.1 select_reduce_fusion
  8.0 0.8 select_reduce_fusion.1
  8.8 1.3 multiply_convert_fusion
  10.1 0.2 conditional.5
  10.1 0.2 broadcast.64
  10.3 1.3 copy-done.2
  11.7 150.1 %all-reduce.3.cloned.1.call-done = bf16[1152,896]{1,0:T(8,128)(2,1)} async-done(((bf16[1152,896]{1,0:T(8,128)(2,1)}), bf16[1152,896]{1,0:T(8,128)(2,1)}) %all-reduce.3.cloned.1.call-update) | async-done | bytes 2064400 | tf_op jit(solution)/shard_map/psum | solution.py:96
  161.8 5.8 %fusion.3 = (bf16[1152,896]{1,0:T(8,128)(2,1)}, bf16[1152,896]{1,0:T(8,128)(2,1)S(1)}, bf16[1152,896]{1,0:T(8,128)(2,1)}) fusion(bf16[1152,896]{1,0:T(8,128)(2,1)} %param.28, bf16[1152,896]{1,0:T(8,128)(2,1)} %param.27, bf16[1152,896]{1,0:T(8,128)(2,1)} %all-reduce.3.cloned.1.call-done), kind=kLoop, calls=%fused_computation.10 | loop fusion | flops 19611648 | bytes 12386304 | tf_op jit(solution)/shard_map/convert_element_type | solution.py:88
  167.6 0.8 copy-done.3
  168.5 0.8 conditional.9
  168.5 0.8 broadcast.67
  169.3 1.0 slice.39
  170.3 9.2 %collective-permute-start.4 = (bf16[896,128]{1,0:T(8,128)(2,1)S(1)}, bf16[896,128]{1,0:T(8,128)(2,1)}, u32[]{:S(2)}, u32[]{:S(2)}) collective-permute-start(bf16[896,128]{1,0:T(8,128)(2,1)S(1)} %slice.39), channel_id=1, source_target_pairs={{0,16},{16,0},{1,17},{17,1},{2,18},{18,2},{3,19},{19,3},{4,20},{20... | collective-permute-start | bytes 688136 | tf_op jit(solution)/shard_map/ppermute | solution.py:20
  179.5 118.6 %all-reduce.5.cloned.1.call-done = bf16[1152,256]{1,0:T(8,128)(2,1)} async-done(((bf16[1152,256]{1,0:T(8,128)(2,1)}), bf16[1152,256]{1,0:T(8,128)(2,1)}) %all-reduce.5.cloned.1.call-update) | async-done | bytes 589840 | tf_op jit(solution)/shard_map/psum | solution.py:124
  298.1 1.3 fusion.13
  299.4 30.8 %psum.23 = f32[1152]{0:T(1024)S(1)} all-reduce(f32[1152]{0:T(1024)S(1)} %fusion.13), channel_id=1, replica_groups=mesh['dp'=16,'segment'=2,'tensor'=16] {'dp'}, use_global_device_ids=true, to_apply=%region_9.10 | all-reduce | flops 1152 | bytes 9216 | tf_op jit(solution)/shard_map/psum | solution.py:44
  330.3 2.7 fusion.15
  333.0 0.1 conditional.8
  333.1 5.9 %collective-permute-start.3 = (bf16[128,896]{1,0:T(8,128)(2,1)S(1)}, bf16[128,896]{1,0:T(8,128)(2,1)S(1)}, u32[]{:S(2)}, u32[]{:S(2)}) collective-permute-start(bf16[128,896]{1,0:T(8,128)(2,1)S(1)} %slice.37), channel_id=1, source_target_pairs={{0,16},{16,0},{1,17},{17,1},{2,18},{18,2},{3,19},{19,3},{4,20},{20... | collective-permute-start | bytes 688136 | tf_op jit(solution)/shard_map/ppermute | solution.py:20
  339.1 1.4 collective-permute-start
  340.5 1.8 slice_select_fusion
  342.3 6.0 %collective-permute-start.2 = (bf16[128,896]{1,0:T(8,128)(2,1)S(1)}, bf16[128,896]{1,0:T(8,128)(2,1)S(1)}, u32[]{:S(2)}, u32[]{:S(2)}) collective-permute-start(bf16[128,896]{1,0:T(8,128)(2,1)S(1)} %slice.35), channel_id=1, source_target_pairs={{0,16},{16,0},{1,17},{17,1},{2,18},{18,2},{3,19},{19,3},{4,20},{20... | collective-permute-start | bytes 688136 | tf_op jit(solution)/shard_map/ppermute | solution.py:20
  348.3 0.7 slice_select_fusion.1
  349.0 10.0 %collective-permute-done.2 = bf16[128,896]{1,0:T(8,128)(2,1)S(1)} collective-permute-done((bf16[128,896]{1,0:T(8,128)(2,1)S(1)}, bf16[128,896]{1,0:T(8,128)(2,1)S(1)}, u32[]{:S(2)}, u32[]{:S(2)}) %collective-permute-start.2) | collective-permute-done | bytes 229408 | tf_op jit(solution)/shard_map/ppermute | solution.py:20
  359.0 0.7 slice_select_fusion.2
  359.8 0.4 conditional.7
  359.8 0.4 fusion.27
  360.2 1.9 collective-permute-start.1
  362.1 0.6 constant_dynamic-slice_fusion
  362.8 5.1 %collective-permute-done.1 = bf16[256,128]{1,0:T(8,128)(2,1)S(1)} collective-permute-done((bf16[256,128]{1,0:T(8,128)(2,1)S(1)}, bf16[256,128]{1,0:T(8,128)(2,1)S(1)}, u32[]{:S(2)}, u32[]{:S(2)}) %collective-permute-start.1) | collective-permute-done | bytes 65568 | tf_op jit(solution)/shard_map/ppermute | solution.py:20
  367.9 0.6 slice_select_fusion.3
  (34 shorter events, 0.5 us)
Async XLA Ops:
  7.2 154.6 %all-reduce.3.cloned.1.call-start = ((), (), s32[]{:S(2)}) async-start(), calls=%async_computation | async-start | bytes 4128768 | tf_op jit(solution)/shard_map/psum | solution.py:96
  10.3 1.3 copy-start.2
  11.6 286.5 %all-reduce.5.cloned.1.call-start = ((), (), s32[]{:S(2)}) async-start(), calls=%async_computation.1 | async-start | bytes 1179648 | tf_op jit(solution)/shard_map/psum | solution.py:124
  167.6 0.8 copy-start.3
  168.4 129.7 %copy-start.5 = (bf16[1152,256]{1,0:T(8,128)(2,1)S(1)}, bf16[1152,256]{1,0:T(8,128)(2,1)}, u32[]{:S(2)}) copy-start(bf16[1152,256]{1,0:T(8,128)(2,1)} %param.24) | copy-start | bytes 1769476
  168.4 129.7 %copy-start.9 = (f32[256]{0:T(256)S(1)}, f32[256]{0:T(256)}, u32[]{:S(2)}) copy-start(f32[256]{0:T(256)} %param.26) | copy-start | bytes 3076
  168.4 161.8 %copy-start.8 = (f32[1152]{0:T(1024)S(1)}, f32[1152]{0:T(1024)}, u32[]{:S(2)}) copy-start(f32[1152]{0:T(1024)} %param.25) | copy-start | bytes 13828
  169.3 161.0 %copy-start.4 = (bf16[1152,256]{1,0:T(8,128)(2,1)S(1)}, bf16[1152,256]{1,0:T(8,128)(2,1)}, u32[]{:S(2)}) copy-start(bf16[1152,256]{1,0:T(8,128)(2,1)} %param.29) | copy-start | bytes 1769476
  170.3 170.2 %collective-permute-start.4 = (bf16[896,128]{1,0:T(8,128)(2,1)S(1)}, bf16[896,128]{1,0:T(8,128)(2,1)}, u32[]{:S(2)}, u32[]{:S(2)}) collective-permute-start(bf16[896,128]{1,0:T(8,128)(2,1)S(1)} %slice.39), channel_id=1, source_target_pairs={{0,16},{16,0},{1,17},{17,1},{2,18},{18,2},{3,19},{19,3},{4,20},{20... | collective-permute-start | bytes 688136 | tf_op jit(solution)/shard_map/ppermute | solution.py:20
  330.2 2.7 copy-start
  333.0 6.1 %copy-start.6 = (bf16[1152,256]{1,0:T(8,128)(2,1)S(1)}, bf16[1152,256]{1,0:T(8,128)(2,1)}, u32[]{:S(2)}) copy-start(bf16[1152,256]{1,0:T(8,128)(2,1)} %get-tuple-element.72) | copy-start | bytes 1769476
  333.1 15.2 %collective-permute-start.3 = (bf16[128,896]{1,0:T(8,128)(2,1)S(1)}, bf16[128,896]{1,0:T(8,128)(2,1)S(1)}, u32[]{:S(2)}, u32[]{:S(2)}) collective-permute-start(bf16[128,896]{1,0:T(8,128)(2,1)S(1)} %slice.37), channel_id=1, source_target_pairs={{0,16},{16,0},{1,17},{17,1},{2,18},{18,2},{3,19},{19,3},{4,20},{20... | collective-permute-start | bytes 688136 | tf_op jit(solution)/shard_map/ppermute | solution.py:20
  339.1 20.7 %copy-start.10 = (bf16[1152,256]{1,0:T(8,128)(2,1)S(1)}, bf16[1152,256]{1,0:T(8,128)(2,1)}, u32[]{:S(2)}) copy-start(bf16[1152,256]{1,0:T(8,128)(2,1)} %param.23) | copy-start | bytes 1769476
  339.1 20.7 %collective-permute-start = (bf16[1152,256]{1,0:T(8,128)(2,1)S(1)}, bf16[1152,256]{1,0:T(8,128)(2,1)S(1)}, u32[]{:S(2)}, u32[]{:S(2)}) collective-permute-start(bf16[1152,256]{1,0:T(8,128)(2,1)S(1)} %copy-done.6), channel_id=1, source_target_pairs={{16,0},{17,1},{18,2},{19,3},{20,4},{21,5},{22,6},{23,7},{24,8},{25... | collective-permute-start | bytes 1769480 | tf_op jit(solution)/shard_map/ppermute | solution.py:14
  342.3 16.7 %collective-permute-start.2 = (bf16[128,896]{1,0:T(8,128)(2,1)S(1)}, bf16[128,896]{1,0:T(8,128)(2,1)S(1)}, u32[]{:S(2)}, u32[]{:S(2)}) collective-permute-start(bf16[128,896]{1,0:T(8,128)(2,1)S(1)} %slice.35), channel_id=1, source_target_pairs={{0,16},{16,0},{1,17},{17,1},{2,18},{18,2},{3,19},{19,3},{4,20},{20... | collective-permute-start | bytes 688136 | tf_op jit(solution)/shard_map/ppermute | solution.py:20
  360.2 7.7 %collective-permute-start.1 = (bf16[256,128]{1,0:T(8,128)(2,1)S(1)}, bf16[256,128]{1,0:T(8,128)(2,1)S(1)}, u32[]{:S(2)}, u32[]{:S(2)}) collective-permute-start(bf16[256,128]{1,0:T(8,128)(2,1)S(1)} %slice.32), channel_id=1, source_target_pairs={{0,16},{16,0},{1,17},{17,1},{2,18},{18,2},{3,19},{19,3},{4,20},{20... | collective-permute-start | bytes 196616 | tf_op jit(solution)/shard_map/ppermute | solution.py:20
Sparse Core Ops, SparseCore 0:
  11.7 149.9 all-reduce.2
  168.5 129.4 all-reduce.4
where the time goes:
time: 376 us; the launch traced here: 375 us
  waiting for transfers between devices  284 us (76%)
  blocking collectives  30.8 us (8%)
  starting transfers between devices  24.5 us (7%)
  other arithmetic  16.6 us (4%)
  between operations  14.3 us (4%)
  local copies, waits for them, and re-layouts  4.94 us (1%)
    psum x1, waiting for transfers between devices, shards(): lax.psum(lax.cond(ffn_side, lambda: jnp.einsum('td,fd->tf', weighted, dow...  150 us
    psum x1, waiting for transfers between devices, shards(): lax.psum(lax.cond(ffn_side, product, lambda: jnp.zeros((total_rows, featu...  119 us
    psum x1, blocking collectives, row_statistic(): return lax.psum(partial_dot, 'dp')  30.8 us
    ppermute x4, starting transfers between devices, from_partner(): return lax.ppermute(value, axis, pairs)  23 us
    ppermute x4, waiting for transfers between devices, from_partner(): return lax.ppermute(value, axis, pairs)  15.1 us
  transfers between devices with their start and end apart: 7, of which 4 were waited for; matrix products, arithmetic and copies ran while one was open for 3% of the time, Pallas kernels for 0%

commit v1 on v0

--- a/solution.py
+++ b/solution.py
@@ -121,11 +121,14 @@
             "tf,df->td", up_delta, up_weight, preferred_element_type=jnp.float32
         )
 
-    normed_delta = lax.psum(
-        lax.cond(ffn_side, product, lambda: jnp.zeros((total_rows, features), jnp.float32)).astype(
-            jnp.bfloat16
+    normed_delta = jnp.sum(
+        lax.all_gather(
+            lax.cond(
+                ffn_side, product, lambda: jnp.zeros((total_rows, features), jnp.float32)
+            ).astype(jnp.bfloat16),
+            "tensor",
         ),
-        "tensor",
+        axis=0,
     ).astype(jnp.float32)
     grad_every = finish_rows(weighted, residual, inverse_rms, norm_gain, normed_delta)
     arrived = shifted(grad_every, "segment", -1)

time: 376 us -> 317 us (0.84)
  the two profiles are of different devices: /device:TPU:14 before, /device:TPU:2 now
where the time goes in v1:
time: 317 us; the launch traced here: 316 us
  waiting for transfers between devices  218 us (69%)
  blocking collectives  31.8 us (10%)
  starting transfers between devices  26 us (8%)
  other arithmetic  22 us (7%)
  between operations  14.3 us (5%)
    psum x1, waiting for transfers between devices, shards(): lax.psum(lax.cond(ffn_side, lambda: jnp.einsum('td,fd->tf', weighted, dow...  150 us
    all_gather x1, waiting for transfers between devices, shards(): lax.all_gather(lax.cond(ffn_side, product, lambda: jnp.zeros((total_rows,...  53.5 us
    psum x1, blocking collectives, row_statistic(): return lax.psum(partial_dot, 'dp')  31.8 us
    ppermute x4, starting transfers between devices, from_partner(): return lax.ppermute(value, axis, pairs)  24.5 us
    ppermute x4, waiting for transfers between devices, from_partner(): return lax.ppermute(value, axis, pairs)  14.6 us
  transfers between devices with their start and end apart: 7, of which 4 were waited for; matrix products, arithmetic and copies ran while one was open for 4% of the time, Pallas kernels for 0%

profile of v1, /device:TPU:2, one launch (start us, length us, event | category | flops | bytes accessed | tf_op | source)
XLA Modules:
  0.0 316.1 jit_solution(14834627990252211231)
XLA Ops:
  7.2 0.7 divide_multiply_fusion
  7.9 0.1 select_reduce_fusion
  8.0 0.8 select_reduce_fusion.1
  8.8 1.3 multiply_convert_fusion
  10.1 0.2 conditional.5
  10.1 0.2 broadcast.64
  10.3 1.3 copy-done.2
  11.6 150.2 %all-reduce.2.cloned.1.call-done = bf16[1152,896]{1,0:T(8,128)(2,1)} async-done(((bf16[1152,896]{1,0:T(8,128)(2,1)}), bf16[1152,896]{1,0:T(8,128)(2,1)}) %all-reduce.2.cloned.1.call-update) | async-done | bytes 2064400 | tf_op jit(solution)/shard_map/psum | solution.py:96
  161.8 5.8 %fusion.3 = (bf16[1152,896]{1,0:T(8,128)(2,1)}, bf16[1152,896]{1,0:T(8,128)(2,1)S(1)}, bf16[1152,896]{1,0:T(8,128)(2,1)}) fusion(bf16[1152,896]{1,0:T(8,128)(2,1)} %param.28, bf16[1152,896]{1,0:T(8,128)(2,1)} %param.27, bf16[1152,896]{1,0:T(8,128)(2,1)} %all-reduce.2.cloned.1.call-done), kind=kLoop, calls=%fused_computation.10 | loop fusion | flops 19611648 | bytes 12386304 | tf_op jit(solution)/shard_map/convert_element_type | solution.py:88
  167.7 0.8 copy-done.3
  168.5 0.1 conditional.9
  168.6 10.1 %collective-permute-start.4 = (bf16[896,128]{1,0:T(8,128)(2,1)S(1)}, bf16[896,128]{1,0:T(8,128)(2,1)}, u32[]{:S(2)}, u32[]{:S(2)}) collective-permute-start(bf16[896,128]{1,0:T(8,128)(2,1)S(1)} %slice.39), channel_id=1, source_target_pairs={{0,16},{16,0},{1,17},{17,1},{2,18},{18,2},{3,19},{19,3},{4,20},{20... | collective-permute-start | bytes 688136 | tf_op jit(solution)/shard_map/ppermute | solution.py:20
  178.7 53.5 %all-gather.3.cloned.1.call-done = bf16[18432,256]{1,0:T(8,128)(2,1)} async-done(((bf16[1152,256]{1,0:T(8,128)(2,1)}), bf16[18432,256]{1,0:T(8,128)(2,1)}) %all-gather.3.cloned.1.call-update) | async-done | bytes 9437200 | tf_op jit(solution)/shard_map/all_gather | solution.py:125
  232.3 5.4 %reduce_sum.41 = bf16[1152,256]{1,0:T(8,128)(2,1)S(1)} reduce(bf16[16,1152,256]{2,1,0:T(8,128)(2,1)} %bitcast.15, bf16[]{:T(256)} %constant.56.clone.1), dimensions={0}, to_apply=%region_7.8 | reduce | flops 4423680 | bytes 10027010 | tf_op jit(solution)/shard_map/reduce_sum | solution.py:124
  237.7 1.3 fusion.13
  239.0 31.8 %psum.15 = f32[1152]{0:T(1024)S(1)} all-reduce(f32[1152]{0:T(1024)S(1)} %fusion.13), channel_id=1, replica_groups=mesh['dp'=16,'segment'=2,'tensor'=16] {'dp'}, use_global_device_ids=true, to_apply=%region_9.10 | all-reduce | flops 1152 | bytes 9216 | tf_op jit(solution)/shard_map/psum | solution.py:44
  270.8 2.7 fusion.15
  273.5 0.1 conditional.8
  273.6 6.6 %collective-permute-start.3 = (bf16[128,896]{1,0:T(8,128)(2,1)S(1)}, bf16[128,896]{1,0:T(8,128)(2,1)S(1)}, u32[]{:S(2)}, u32[]{:S(2)}) collective-permute-start(bf16[128,896]{1,0:T(8,128)(2,1)S(1)} %slice.37), channel_id=1, source_target_pairs={{0,16},{16,0},{1,17},{17,1},{2,18},{18,2},{3,19},{19,3},{4,20},{20... | collective-permute-start | bytes 688136 | tf_op jit(solution)/shard_map/ppermute | solution.py:20
  280.2 1.4 collective-permute-start
  281.7 1.8 slice_select_fusion
  283.5 6.0 %collective-permute-start.2 = (bf16[128,896]{1,0:T(8,128)(2,1)S(1)}, bf16[128,896]{1,0:T(8,128)(2,1)S(1)}, u32[]{:S(2)}, u32[]{:S(2)}) collective-permute-start(bf16[128,896]{1,0:T(8,128)(2,1)S(1)} %slice.35), channel_id=1, source_target_pairs={{0,16},{16,0},{1,17},{17,1},{2,18},{18,2},{3,19},{19,3},{4,20},{20... | collective-permute-start | bytes 688136 | tf_op jit(solution)/shard_map/ppermute | solution.py:20
  289.5 0.7 slice_select_fusion.1
  290.2 9.5 %collective-permute-done.2 = bf16[128,896]{1,0:T(8,128)(2,1)S(1)} collective-permute-done((bf16[128,896]{1,0:T(8,128)(2,1)S(1)}, bf16[128,896]{1,0:T(8,128)(2,1)S(1)}, u32[]{:S(2)}, u32[]{:S(2)}) %collective-permute-start.2) | collective-permute-done | bytes 229408 | tf_op jit(solution)/shard_map/ppermute | solution.py:20
  299.7 0.7 slice_select_fusion.2
  300.4 0.1 broadcast_select_fusion
  300.5 0.4 conditional.7
  300.5 0.4 fusion.27
  300.9 1.9 collective-permute-start.1
  302.9 0.6 constant_dynamic-slice_fusion
  303.5 5.1 %collective-permute-done.1 = bf16[256,128]{1,0:T(8,128)(2,1)S(1)} collective-permute-done((bf16[256,128]{1,0:T(8,128)(2,1)S(1)}, bf16[256,128]{1,0:T(8,128)(2,1)S(1)}, u32[]{:S(2)}, u32[]{:S(2)}) %collective-permute-start.1) | collective-permute-done | bytes 65568 | tf_op jit(solution)/shard_map/ppermute | solution.py:20
  308.6 0.6 slice_select_fusion.3
  (35 shorter events, 0.4 us)
Async XLA Ops:
  7.2 154.7 %all-reduce.2.cloned.1.call-start = ((), (), s32[]{:S(2)}) async-start(), calls=%async_computation | async-start | bytes 4128768 | tf_op jit(solution)/shard_map/psum | solution.py:96
  10.3 1.3 copy-start.2
  11.6 220.7 %all-gather.3.cloned.1.call-start = ((), (), s32[]{:S(2)}) async-start(), calls=%async_computation.1 | async-start | bytes 10027008 | tf_op jit(solution)/shard_map/all_gather | solution.py:125
  167.7 0.8 copy-start.3
  168.6 63.6 %copy-start.6 = (bf16[896,256]{1,0:T(8,128)(2,1)}, bf16[896,256]{1,0:T(8,128)(2,1)S(1)}, u32[]{:S(2)}) copy-start(bf16[896,256]{1,0:T(8,128)(2,1)S(1)} %get-tuple-element.80) | copy-start | bytes 1376260
  168.6 113.0 %collective-permute-start.4 = (bf16[896,128]{1,0:T(8,128)(2,1)S(1)}, bf16[896,128]{1,0:T(8,128)(2,1)}, u32[]{:S(2)}, u32[]{:S(2)}) collective-permute-start(bf16[896,128]{1,0:T(8,128)(2,1)S(1)} %slice.39), channel_id=1, source_target_pairs={{0,16},{16,0},{1,17},{17,1},{2,18},{18,2},{3,19},{19,3},{4,20},{20... | collective-permute-start | bytes 688136 | tf_op jit(solution)/shard_map/ppermute | solution.py:20
  232.3 5.4 %copy-start.9 = (f32[256]{0:T(256)S(1)}, f32[256]{0:T(256)}, u32[]{:S(2)}) copy-start(f32[256]{0:T(256)} %param.26) | copy-start | bytes 3076
  232.3 38.5 %copy-start.8 = (f32[1152]{0:T(1024)S(1)}, f32[1152]{0:T(1024)}, u32[]{:S(2)}) copy-start(f32[1152]{0:T(1024)} %param.25) | copy-start | bytes 13828
  232.3 38.6 %copy-start.4 = (bf16[1152,256]{1,0:T(8,128)(2,1)S(1)}, bf16[1152,256]{1,0:T(8,128)(2,1)}, u32[]{:S(2)}) copy-start(bf16[1152,256]{1,0:T(8,128)(2,1)} %param.29) | copy-start | bytes 1769476
  270.8 2.7 copy-start
  273.5 6.7 %copy-start.5 = (bf16[1152,256]{1,0:T(8,128)(2,1)S(1)}, bf16[1152,256]{1,0:T(8,128)(2,1)}, u32[]{:S(2)}) copy-start(bf16[1152,256]{1,0:T(8,128)(2,1)} %get-tuple-element.72) | copy-start | bytes 1769476
  273.6 15.8 %collective-permute-start.3 = (bf16[128,896]{1,0:T(8,128)(2,1)S(1)}, bf16[128,896]{1,0:T(8,128)(2,1)S(1)}, u32[]{:S(2)}, u32[]{:S(2)}) collective-permute-start(bf16[128,896]{1,0:T(8,128)(2,1)S(1)} %slice.37), channel_id=1, source_target_pairs={{0,16},{16,0},{1,17},{17,1},{2,18},{18,2},{3,19},{19,3},{4,20},{20... | collective-permute-start | bytes 688136 | tf_op jit(solution)/shard_map/ppermute | solution.py:20
  280.2 20.3 %copy-start.10 = (bf16[1152,256]{1,0:T(8,128)(2,1)S(1)}, bf16[1152,256]{1,0:T(8,128)(2,1)}, u32[]{:S(2)}) copy-start(bf16[1152,256]{1,0:T(8,128)(2,1)} %param.23) | copy-start | bytes 1769476
  280.2 20.2 %collective-permute-start = (bf16[1152,256]{1,0:T(8,128)(2,1)S(1)}, bf16[1152,256]{1,0:T(8,128)(2,1)S(1)}, u32[]{:S(2)}, u32[]{:S(2)}) collective-permute-start(bf16[1152,256]{1,0:T(8,128)(2,1)S(1)} %copy-done.5), channel_id=1, source_target_pairs={{16,0},{17,1},{18,2},{19,3},{20,4},{21,5},{22,6},{23,7},{24,8},{25... | collective-permute-start | bytes 1769480 | tf_op jit(solution)/shard_map/ppermute | solution.py:14
  283.5 16.2 %collective-permute-start.2 = (bf16[128,896]{1,0:T(8,128)(2,1)S(1)}, bf16[128,896]{1,0:T(8,128)(2,1)S(1)}, u32[]{:S(2)}, u32[]{:S(2)}) collective-permute-start(bf16[128,896]{1,0:T(8,128)(2,1)S(1)} %slice.35), channel_id=1, source_target_pairs={{0,16},{16,0},{1,17},{17,1},{2,18},{18,2},{3,19},{19,3},{4,20},{20... | collective-permute-start | bytes 688136 | tf_op jit(solution)/shard_map/ppermute | solution.py:20
  300.9 7.7 %collective-permute-start.1 = (bf16[256,128]{1,0:T(8,128)(2,1)S(1)}, bf16[256,128]{1,0:T(8,128)(2,1)S(1)}, u32[]{:S(2)}, u32[]{:S(2)}) collective-permute-start(bf16[256,128]{1,0:T(8,128)(2,1)S(1)} %slice.32), channel_id=1, source_target_pairs={{0,16},{16,0},{1,17},{17,1},{2,18},{18,2},{3,19},{19,3},{4,20},{20... | collective-permute-start | bytes 196616 | tf_op jit(solution)/shard_map/ppermute | solution.py:20
Sparse Core Ops, SparseCore 0:
  11.7 150.0 all-reduce.1
  168.7 63.5 all-gather.2
